TPU v7x, 512 devices: a whole 4x4x16 slice. The times are simulated.
512 devices in a mesh: ctx: 32 (over z, core), ch: 16 (over x, y).
Axes of the slice: x: 4, y: 4, z: 16, core: 2. Of those that a mesh axis runs over, the one named last changes fastest.
Arguments:
- signal: bfloat16 [4096, 8192], P('ctx', 'ch'), may hold values from -170 to 170, as said below
- norm_gain: float32 [8192], P('ch'), may hold values from 0.1 to 1.9
- skip_gain: float32 [8192], P('ch'), may hold values from 0.5 to 1.5
- filter_taps: bfloat16 [4096, 8192], P('ctx', 'ch'), may hold values from -1.5 to 1.5, as said below
- out_gate: bfloat16 [4096, 8192], P('ctx', 'ch'), may hold values from -6 to 6
Outputs:
- mixture: bfloat16 [4096, 8192], P('ctx', 'ch')
Inputs may be any that keep to these rules, and one draw needn't show every extreme that they name: `signal`: features whose channels and tokens have different scales. `filter_taps`: a filter whose taps fall off along the lags at a rate that differs between channels.
All inputs are finite; a program needn't handle non-finite values.
Results may differ from a plain program's by a relative error of at most 0.006.
Values may be sent and summed in bfloat16 or wider, within the bound.
A program may use at most 64 MiB of HBM per device.

v0:
```python
import math
import jax
import jax.numpy as jnp
from jax import lax
from jax.sharding import PartitionSpec as P

C = 8192
EPS = 1e-06


def passed_along(block, axis, distance):
    devices = range(lax.axis_size(axis))
    route = [(i - distance, i) for i in devices if i - distance in devices]
    return lax.ppermute(block, axis, route)


def split_parts(matrix):
    high = matrix.astype(jnp.bfloat16)
    kept = lax.optimization_barrier(high)
    low = (matrix - kept.astype(jnp.float32)).astype(jnp.bfloat16)
    return (high, low)


def table_dot(table_pair, data):
    return jnp.dot(table_pair[0], data, preferred_element_type=jnp.float32) + jnp.dot(
        table_pair[1], data, preferred_element_type=jnp.float32
    )


def fine_dot(table_pair, data):
    data_high, data_low = split_parts(data)
    return (
        jnp.dot(table_pair[0], data_high, preferred_element_type=jnp.float32)
        + jnp.dot(table_pair[0], data_low, preferred_element_type=jnp.float32)
        + jnp.dot(table_pair[1], data_high, preferred_element_type=jnp.float32)
    )


def dft_tables(tok_rows):
    freq_ids = jnp.arange(tok_rows + 1, dtype=jnp.int32)
    row_ids = jnp.arange(tok_rows, dtype=jnp.int32)
    out_ids = jnp.arange(2 * tok_rows, dtype=jnp.int32)
    fwd_phase = (freq_ids[:, None] * row_ids[None, :] % (2 * tok_rows)).astype(jnp.float32) * (
        math.pi / tok_rows
    )
    inv_phase = (out_ids[:, None] * freq_ids[None, :] % (2 * tok_rows)).astype(jnp.float32) * (
        math.pi / tok_rows
    )
    weights = jnp.where((freq_ids == 0) | (freq_ids == tok_rows), 1.0, 2.0).astype(jnp.float32) / (
        2.0 * tok_rows
    )
    return (
        jnp.cos(fwd_phase),
        jnp.sin(fwd_phase),
        jnp.cos(inv_phase) * weights[None, :],
        jnp.sin(inv_phase) * weights[None, :],
    )


def local(signal, norm_gain, skip_gain, filter_taps, out_gate):
    tok_rows, channels = signal.shape
    ctx_count = lax.axis_size("ctx")
    ctx_index = lax.axis_index("ctx")
    values = signal.astype(jnp.float32)
    row_power = lax.psum(jnp.sum(values * values, axis=1), "ch") / C
    normed = (values * lax.rsqrt(row_power + EPS)[:, None] * norm_gain[None, :]).astype(
        jnp.bfloat16
    )
    fwd_cos, fwd_sin, inv_cos, inv_sin = dft_tables(tok_rows)
    cos_high, cos_low = split_parts(fwd_cos)
    sin_high, sin_low = split_parts(fwd_sin)
    halfway = ctx_count // 2
    quarter = ctx_count // 4
    helper = jnp.zeros((), jnp.bool_)
    first_own = jnp.zeros((), jnp.int32)
    partner = ctx_index + halfway
    whole_filter = lax.all_gather(filter_taps, "ctx", axis=0, tiled=True)

    def spectrum(segment):
        span_rows = segment.shape[0]
        cos_pair = (cos_high, cos_low)
        sin_pair = (sin_high, sin_low)
        return (table_dot(cos_pair, segment), -table_dot(sin_pair, segment))

    def lag_product(lag_block, sig_re, sig_im, sum_re, sum_im):
        taps = lax.dynamic_slice_in_dim(whole_filter, lag_block * tok_rows, tok_rows, 0)
        fil_re, fil_im = spectrum(taps)
        return (
            sum_re + fil_re * sig_re - fil_im * sig_im,
            sum_im + fil_re * sig_im + fil_im * sig_re,
        )

    blank = jnp.zeros((tok_rows + 1, channels), jnp.float32)
    segment_in = lax.all_gather(normed, "ctx", axis=0, tiled=True)
    span_rows = min(segment_in.shape[0], tok_rows)

    def one_span(sub_index, running):
        anchor = sub_index * span_rows
        segment = lax.dynamic_slice_in_dim(segment_in, sub_index * span_rows, span_rows, 0)
        source = anchor // tok_rows
        own_ok = (source <= ctx_index) & (source >= first_own)
        help_ok = helper & (source < quarter)

        def do_work(state):
            sig_re, sig_im = spectrum(segment)

            def own_add(pair_in):
                return lag_product(ctx_index - source, sig_re, sig_im, pair_in[0], pair_in[1])

            def help_add(pair_in):
                return lag_product(partner - source, sig_re, sig_im, pair_in[0], pair_in[1])

            def keep_pair(pair_in):
                return pair_in

            own_re, own_im = lax.cond(own_ok, own_add, keep_pair, (state[0], state[1]))
            help_re, help_im = lax.cond(help_ok, help_add, keep_pair, (state[2], state[3]))
            return (own_re, own_im, help_re, help_im)

        def skip_work(state):
            return state

        return lax.cond(own_ok | help_ok, do_work, skip_work, running)

    own_re, own_im, help_re, help_im = lax.fori_loop(
        0, segment_in.shape[0] // span_rows, one_span, (blank, blank, blank, blank)
    )
    low_cos = split_parts(inv_cos[:tok_rows])
    low_sin = split_parts(inv_sin[:tok_rows])
    high_cos = split_parts(inv_cos[tok_rows:])
    high_sin = split_parts(inv_sin[tok_rows:])
    low_part = fine_dot(low_cos, own_re) - fine_dot(low_sin, own_im)
    high_part = fine_dot(high_cos, own_re) - fine_dot(high_sin, own_im)
    convolved = low_part + passed_along(high_part.astype(jnp.bfloat16), "ctx", 1).astype(
        high_part.dtype
    )
    mixture = out_gate.astype(jnp.float32) * (
        convolved + skip_gain[None, :] * normed.astype(jnp.float32)
    )
    return mixture.astype(jnp.bfloat16)


def solution(mesh):
    return jax.shard_map(
        local,
        mesh=mesh,
        in_specs=(P("ctx", "ch"), P("ch"), P("ch"), P("ctx", "ch"), P("ctx", "ch")),
        out_specs=P("ctx", "ch"),
        check_vma=False,
    )
```

profile of v0, /device:TPU:483, one launch (start us, length us, event | category | flops | bytes accessed | tf_op | source)
XLA Modules:
  0.0 462.2 jit_solution(6223332939443053521)
XLA Ops:
  8.3 28.1 %psum.7 = f32[128]{0:T(128)S(1)} all-reduce(f32[128]{0:T(128)S(1)} %fusion.33), channel_id=1, replica_groups=mesh['ctx'=32,'ch'=16] {'ch'}, use_global_device_ids=true, to_apply=%region_1.0 | all-reduce | flops 128 | bytes 1024 | tf_op jit(solution)/shard_map/psum | solution.py:65
  40.1 41.6 %all-gather.5.cloned.1.call-done = bf16[4096,512]{1,0:T(8,128)(2,1)} async-done(((bf16[128,512]{1,0:T(8,128)(2,1)}), bf16[4096,512]{1,0:T(8,128)(2,1)}) %all-gather.5.cloned.1.call-update) | async-done | bytes 4194320 | tf_op jit(solution)/shard_map/all_gather | solution.py:77
  81.7 72.9 %all-gather.3.cloned.1.call-done = bf16[4096,512]{1,0:T(8,128)(2,1)} async-done(((bf16[128,512]{1,0:T(8,128)(2,1)}), bf16[4096,512]{1,0:T(8,128)(2,1)}) %all-gather.3.cloned.1.call-update) | async-done | bytes 4194320 | tf_op jit(solution)/shard_map/all_gather | solution.py:94
  154.6 294.8 %while.19 = (s32[]{:T(128)}, f32[129,512]{1,0:T(8,128)S(1)}, f32[129,512]{1,0:T(8,128)S(1)}, s32[]{:T(128)}, bf16[4096,512]{1,0:T(8,128)(2,1)}, /*index=5*/bf16[...) while((s32[]{:T(128)}, f32[129,512]{1,0:T(8,128)S(1)}, ...), condition=%wide.region_7.8_spmd.clone.clone, body=%wide.region_2.7_spmd.clone.clone.sunk | while | flops 136455184 | bytes 6134993 | solution.py:125
  155.0 8.9 %conditional.5 = ((f32[129,512]{1,0:T(8,128)S(1)}, f32[129,512]{1,0:T(8,128)S(1)})) conditional(s32[]{:T(128)} %convert_element_type.331, (f32[129,512]{1,0:T(8,128)S(1)}, f32[129,512]{1,0:T(8,128)S(1)}) %tuple.76, (pred[]{:T(512)}, s32[]{:T(128)}, pred[]{:T(512)}, bf16[4096,512]{1,0:T(8,128)(2,1)}, bf16[129,128]{1,0:T(8,128)(2,1)S(1)}, ...), branch_computations={%region_3.3_spmd, %region_4.6_spmd} | conditional | flops 136190976 | bytes 6068488 | solution.py:123
  159.4 4.5 conditional
  164.2 8.9 %conditional.5 = ((f32[129,512]{1,0:T(8,128)S(1)}, f32[129,512]{1,0:T(8,128)S(1)})) conditional(s32[]{:T(128)} %convert_element_type.331, (f32[129,512]{1,0:T(8,128)S(1)}, f32[129,512]{1,0:T(8,128)S(1)}) %tuple.76, (pred[]{:T(512)}, s32[]{:T(128)}, pred[]{:T(512)}, bf16[4096,512]{1,0:T(8,128)(2,1)}, bf16[129,128]{1,0:T(8,128)(2,1)S(1)}, ...), branch_computations={%region_3.3_spmd, %region_4.6_spmd} | conditional | flops 136190976 | bytes 6068488 | solution.py:123
  173.4 8.9 %conditional.5 = ((f32[129,512]{1,0:T(8,128)S(1)}, f32[129,512]{1,0:T(8,128)S(1)})) conditional(s32[]{:T(128)} %convert_element_type.331, (f32[129,512]{1,0:T(8,128)S(1)}, f32[129,512]{1,0:T(8,128)S(1)}) %tuple.76, (pred[]{:T(512)}, s32[]{:T(128)}, pred[]{:T(512)}, bf16[4096,512]{1,0:T(8,128)(2,1)}, bf16[129,128]{1,0:T(8,128)(2,1)S(1)}, ...), branch_computations={%region_3.3_spmd, %region_4.6_spmd} | conditional | flops 136190976 | bytes 6068488 | solution.py:123
  177.8 4.5 conditional
  182.6 8.9 %conditional.5 = ((f32[129,512]{1,0:T(8,128)S(1)}, f32[129,512]{1,0:T(8,128)S(1)})) conditional(s32[]{:T(128)} %convert_element_type.331, (f32[129,512]{1,0:T(8,128)S(1)}, f32[129,512]{1,0:T(8,128)S(1)}) %tuple.76, (pred[]{:T(512)}, s32[]{:T(128)}, pred[]{:T(512)}, bf16[4096,512]{1,0:T(8,128)(2,1)}, bf16[129,128]{1,0:T(8,128)(2,1)S(1)}, ...), branch_computations={%region_3.3_spmd, %region_4.6_spmd} | conditional | flops 136190976 | bytes 6068488 | solution.py:123
  191.8 8.9 %conditional.5 = ((f32[129,512]{1,0:T(8,128)S(1)}, f32[129,512]{1,0:T(8,128)S(1)})) conditional(s32[]{:T(128)} %convert_element_type.331, (f32[129,512]{1,0:T(8,128)S(1)}, f32[129,512]{1,0:T(8,128)S(1)}) %tuple.76, (pred[]{:T(512)}, s32[]{:T(128)}, pred[]{:T(512)}, bf16[4096,512]{1,0:T(8,128)(2,1)}, bf16[129,128]{1,0:T(8,128)(2,1)S(1)}, ...), branch_computations={%region_3.3_spmd, %region_4.6_spmd} | conditional | flops 136190976 | bytes 6068488 | solution.py:123
  201.0 8.9 %conditional.5 = ((f32[129,512]{1,0:T(8,128)S(1)}, f32[129,512]{1,0:T(8,128)S(1)})) conditional(s32[]{:T(128)} %convert_element_type.331, (f32[129,512]{1,0:T(8,128)S(1)}, f32[129,512]{1,0:T(8,128)S(1)}) %tuple.76, (pred[]{:T(512)}, s32[]{:T(128)}, pred[]{:T(512)}, bf16[4096,512]{1,0:T(8,128)(2,1)}, bf16[129,128]{1,0:T(8,128)(2,1)S(1)}, ...), branch_computations={%region_3.3_spmd, %region_4.6_spmd} | conditional | flops 136190976 | bytes 6068488 | solution.py:123
  205.4 4.5 conditional
  210.3 8.9 %conditional.5 = ((f32[129,512]{1,0:T(8,128)S(1)}, f32[129,512]{1,0:T(8,128)S(1)})) conditional(s32[]{:T(128)} %convert_element_type.331, (f32[129,512]{1,0:T(8,128)S(1)}, f32[129,512]{1,0:T(8,128)S(1)}) %tuple.76, (pred[]{:T(512)}, s32[]{:T(128)}, pred[]{:T(512)}, bf16[4096,512]{1,0:T(8,128)(2,1)}, bf16[129,128]{1,0:T(8,128)(2,1)S(1)}, ...), branch_computations={%region_3.3_spmd, %region_4.6_spmd} | conditional | flops 136190976 | bytes 6068488 | solution.py:123
  219.5 8.9 %conditional.5 = ((f32[129,512]{1,0:T(8,128)S(1)}, f32[129,512]{1,0:T(8,128)S(1)})) conditional(s32[]{:T(128)} %convert_element_type.331, (f32[129,512]{1,0:T(8,128)S(1)}, f32[129,512]{1,0:T(8,128)S(1)}) %tuple.76, (pred[]{:T(512)}, s32[]{:T(128)}, pred[]{:T(512)}, bf16[4096,512]{1,0:T(8,128)(2,1)}, bf16[129,128]{1,0:T(8,128)(2,1)S(1)}, ...), branch_computations={%region_3.3_spmd, %region_4.6_spmd} | conditional | flops 136190976 | bytes 6068488 | solution.py:123
  223.8 4.5 conditional
  228.7 8.9 %conditional.5 = ((f32[129,512]{1,0:T(8,128)S(1)}, f32[129,512]{1,0:T(8,128)S(1)})) conditional(s32[]{:T(128)} %convert_element_type.331, (f32[129,512]{1,0:T(8,128)S(1)}, f32[129,512]{1,0:T(8,128)S(1)}) %tuple.76, (pred[]{:T(512)}, s32[]{:T(128)}, pred[]{:T(512)}, bf16[4096,512]{1,0:T(8,128)(2,1)}, bf16[129,128]{1,0:T(8,128)(2,1)S(1)}, ...), branch_computations={%region_3.3_spmd, %region_4.6_spmd} | conditional | flops 136190976 | bytes 6068488 | solution.py:123
  237.9 8.9 %conditional.5 = ((f32[129,512]{1,0:T(8,128)S(1)}, f32[129,512]{1,0:T(8,128)S(1)})) conditional(s32[]{:T(128)} %convert_element_type.331, (f32[129,512]{1,0:T(8,128)S(1)}, f32[129,512]{1,0:T(8,128)S(1)}) %tuple.76, (pred[]{:T(512)}, s32[]{:T(128)}, pred[]{:T(512)}, bf16[4096,512]{1,0:T(8,128)(2,1)}, bf16[129,128]{1,0:T(8,128)(2,1)S(1)}, ...), branch_computations={%region_3.3_spmd, %region_4.6_spmd} | conditional | flops 136190976 | bytes 6068488 | solution.py:123
  242.3 4.5 conditional
  247.1 8.9 %conditional.5 = ((f32[129,512]{1,0:T(8,128)S(1)}, f32[129,512]{1,0:T(8,128)S(1)})) conditional(s32[]{:T(128)} %convert_element_type.331, (f32[129,512]{1,0:T(8,128)S(1)}, f32[129,512]{1,0:T(8,128)S(1)}) %tuple.76, (pred[]{:T(512)}, s32[]{:T(128)}, pred[]{:T(512)}, bf16[4096,512]{1,0:T(8,128)(2,1)}, bf16[129,128]{1,0:T(8,128)(2,1)S(1)}, ...), branch_computations={%region_3.3_spmd, %region_4.6_spmd} | conditional | flops 136190976 | bytes 6068488 | solution.py:123
  256.3 8.9 %conditional.5 = ((f32[129,512]{1,0:T(8,128)S(1)}, f32[129,512]{1,0:T(8,128)S(1)})) conditional(s32[]{:T(128)} %convert_element_type.331, (f32[129,512]{1,0:T(8,128)S(1)}, f32[129,512]{1,0:T(8,128)S(1)}) %tuple.76, (pred[]{:T(512)}, s32[]{:T(128)}, pred[]{:T(512)}, bf16[4096,512]{1,0:T(8,128)(2,1)}, bf16[129,128]{1,0:T(8,128)(2,1)S(1)}, ...), branch_computations={%region_3.3_spmd, %region_4.6_spmd} | conditional | flops 136190976 | bytes 6068488 | solution.py:123
  265.5 8.9 %conditional.5 = ((f32[129,512]{1,0:T(8,128)S(1)}, f32[129,512]{1,0:T(8,128)S(1)})) conditional(s32[]{:T(128)} %convert_element_type.331, (f32[129,512]{1,0:T(8,128)S(1)}, f32[129,512]{1,0:T(8,128)S(1)}) %tuple.76, (pred[]{:T(512)}, s32[]{:T(128)}, pred[]{:T(512)}, bf16[4096,512]{1,0:T(8,128)(2,1)}, bf16[129,128]{1,0:T(8,128)(2,1)S(1)}, ...), branch_computations={%region_3.3_spmd, %region_4.6_spmd} | conditional | flops 136190976 | bytes 6068488 | solution.py:123
  269.9 4.5 conditional
  274.7 8.9 %conditional.5 = ((f32[129,512]{1,0:T(8,128)S(1)}, f32[129,512]{1,0:T(8,128)S(1)})) conditional(s32[]{:T(128)} %convert_element_type.331, (f32[129,512]{1,0:T(8,128)S(1)}, f32[129,512]{1,0:T(8,128)S(1)}) %tuple.76, (pred[]{:T(512)}, s32[]{:T(128)}, pred[]{:T(512)}, bf16[4096,512]{1,0:T(8,128)(2,1)}, bf16[129,128]{1,0:T(8,128)(2,1)S(1)}, ...), branch_computations={%region_3.3_spmd, %region_4.6_spmd} | conditional | flops 136190976 | bytes 6068488 | solution.py:123
  284.0 8.9 %conditional.5 = ((f32[129,512]{1,0:T(8,128)S(1)}, f32[129,512]{1,0:T(8,128)S(1)})) conditional(s32[]{:T(128)} %convert_element_type.331, (f32[129,512]{1,0:T(8,128)S(1)}, f32[129,512]{1,0:T(8,128)S(1)}) %tuple.76, (pred[]{:T(512)}, s32[]{:T(128)}, pred[]{:T(512)}, bf16[4096,512]{1,0:T(8,128)(2,1)}, bf16[129,128]{1,0:T(8,128)(2,1)S(1)}, ...), branch_computations={%region_3.3_spmd, %region_4.6_spmd} | conditional | flops 136190976 | bytes 6068488 | solution.py:123
  288.3 4.5 conditional
  293.2 8.9 %conditional.5 = ((f32[129,512]{1,0:T(8,128)S(1)}, f32[129,512]{1,0:T(8,128)S(1)})) conditional(s32[]{:T(128)} %convert_element_type.331, (f32[129,512]{1,0:T(8,128)S(1)}, f32[129,512]{1,0:T(8,128)S(1)}) %tuple.76, (pred[]{:T(512)}, s32[]{:T(128)}, pred[]{:T(512)}, bf16[4096,512]{1,0:T(8,128)(2,1)}, bf16[129,128]{1,0:T(8,128)(2,1)S(1)}, ...), branch_computations={%region_3.3_spmd, %region_4.6_spmd} | conditional | flops 136190976 | bytes 6068488 | solution.py:123
  302.4 8.9 %conditional.5 = ((f32[129,512]{1,0:T(8,128)S(1)}, f32[129,512]{1,0:T(8,128)S(1)})) conditional(s32[]{:T(128)} %convert_element_type.331, (f32[129,512]{1,0:T(8,128)S(1)}, f32[129,512]{1,0:T(8,128)S(1)}) %tuple.76, (pred[]{:T(512)}, s32[]{:T(128)}, pred[]{:T(512)}, bf16[4096,512]{1,0:T(8,128)(2,1)}, bf16[129,128]{1,0:T(8,128)(2,1)S(1)}, ...), branch_computations={%region_3.3_spmd, %region_4.6_spmd} | conditional | flops 136190976 | bytes 6068488 | solution.py:123
  311.6 8.9 %conditional.5 = ((f32[129,512]{1,0:T(8,128)S(1)}, f32[129,512]{1,0:T(8,128)S(1)})) conditional(s32[]{:T(128)} %convert_element_type.331, (f32[129,512]{1,0:T(8,128)S(1)}, f32[129,512]{1,0:T(8,128)S(1)}) %tuple.76, (pred[]{:T(512)}, s32[]{:T(128)}, pred[]{:T(512)}, bf16[4096,512]{1,0:T(8,128)(2,1)}, bf16[129,128]{1,0:T(8,128)(2,1)S(1)}, ...), branch_computations={%region_3.3_spmd, %region_4.6_spmd} | conditional | flops 136190976 | bytes 6068488 | solution.py:123
  320.8 8.9 %conditional.5 = ((f32[129,512]{1,0:T(8,128)S(1)}, f32[129,512]{1,0:T(8,128)S(1)})) conditional(s32[]{:T(128)} %convert_element_type.331, (f32[129,512]{1,0:T(8,128)S(1)}, f32[129,512]{1,0:T(8,128)S(1)}) %tuple.76, (pred[]{:T(512)}, s32[]{:T(128)}, pred[]{:T(512)}, bf16[4096,512]{1,0:T(8,128)(2,1)}, bf16[129,128]{1,0:T(8,128)(2,1)S(1)}, ...), branch_computations={%region_3.3_spmd, %region_4.6_spmd} | conditional | flops 136190976 | bytes 6068488 | solution.py:123
  330.0 8.9 %conditional.5 = ((f32[129,512]{1,0:T(8,128)S(1)}, f32[129,512]{1,0:T(8,128)S(1)})) conditional(s32[]{:T(128)} %convert_element_type.331, (f32[129,512]{1,0:T(8,128)S(1)}, f32[129,512]{1,0:T(8,128)S(1)}) %tuple.76, (pred[]{:T(512)}, s32[]{:T(128)}, pred[]{:T(512)}, bf16[4096,512]{1,0:T(8,128)(2,1)}, bf16[129,128]{1,0:T(8,128)(2,1)S(1)}, ...), branch_computations={%region_3.3_spmd, %region_4.6_spmd} | conditional | flops 136190976 | bytes 6068488 | solution.py:123
  334.4 4.5 conditional
  339.2 8.9 %conditional.5 = ((f32[129,512]{1,0:T(8,128)S(1)}, f32[129,512]{1,0:T(8,128)S(1)})) conditional(s32[]{:T(128)} %convert_element_type.331, (f32[129,512]{1,0:T(8,128)S(1)}, f32[129,512]{1,0:T(8,128)S(1)}) %tuple.76, (pred[]{:T(512)}, s32[]{:T(128)}, pred[]{:T(512)}, bf16[4096,512]{1,0:T(8,128)(2,1)}, bf16[129,128]{1,0:T(8,128)(2,1)S(1)}, ...), branch_computations={%region_3.3_spmd, %region_4.6_spmd} | conditional | flops 136190976 | bytes 6068488 | solution.py:123
  348.4 8.9 %conditional.5 = ((f32[129,512]{1,0:T(8,128)S(1)}, f32[129,512]{1,0:T(8,128)S(1)})) conditional(s32[]{:T(128)} %convert_element_type.331, (f32[129,512]{1,0:T(8,128)S(1)}, f32[129,512]{1,0:T(8,128)S(1)}) %tuple.76, (pred[]{:T(512)}, s32[]{:T(128)}, pred[]{:T(512)}, bf16[4096,512]{1,0:T(8,128)(2,1)}, bf16[129,128]{1,0:T(8,128)(2,1)S(1)}, ...), branch_computations={%region_3.3_spmd, %region_4.6_spmd} | conditional | flops 136190976 | bytes 6068488 | solution.py:123
  352.8 4.5 conditional
  357.7 8.9 %conditional.5 = ((f32[129,512]{1,0:T(8,128)S(1)}, f32[129,512]{1,0:T(8,128)S(1)})) conditional(s32[]{:T(128)} %convert_element_type.331, (f32[129,512]{1,0:T(8,128)S(1)}, f32[129,512]{1,0:T(8,128)S(1)}) %tuple.76, (pred[]{:T(512)}, s32[]{:T(128)}, pred[]{:T(512)}, bf16[4096,512]{1,0:T(8,128)(2,1)}, bf16[129,128]{1,0:T(8,128)(2,1)S(1)}, ...), branch_computations={%region_3.3_spmd, %region_4.6_spmd} | conditional | flops 136190976 | bytes 6068488 | solution.py:123
  366.9 8.9 %conditional.5 = ((f32[129,512]{1,0:T(8,128)S(1)}, f32[129,512]{1,0:T(8,128)S(1)})) conditional(s32[]{:T(128)} %convert_element_type.331, (f32[129,512]{1,0:T(8,128)S(1)}, f32[129,512]{1,0:T(8,128)S(1)}) %tuple.76, (pred[]{:T(512)}, s32[]{:T(128)}, pred[]{:T(512)}, bf16[4096,512]{1,0:T(8,128)(2,1)}, bf16[129,128]{1,0:T(8,128)(2,1)S(1)}, ...), branch_computations={%region_3.3_spmd, %region_4.6_spmd} | conditional | flops 136190976 | bytes 6068488 | solution.py:123
  376.1 8.9 %conditional.5 = ((f32[129,512]{1,0:T(8,128)S(1)}, f32[129,512]{1,0:T(8,128)S(1)})) conditional(s32[]{:T(128)} %convert_element_type.331, (f32[129,512]{1,0:T(8,128)S(1)}, f32[129,512]{1,0:T(8,128)S(1)}) %tuple.76, (pred[]{:T(512)}, s32[]{:T(128)}, pred[]{:T(512)}, bf16[4096,512]{1,0:T(8,128)(2,1)}, bf16[129,128]{1,0:T(8,128)(2,1)S(1)}, ...), branch_computations={%region_3.3_spmd, %region_4.6_spmd} | conditional | flops 136190976 | bytes 6068488 | solution.py:123
  380.5 4.5 conditional
  385.3 8.9 %conditional.5 = ((f32[129,512]{1,0:T(8,128)S(1)}, f32[129,512]{1,0:T(8,128)S(1)})) conditional(s32[]{:T(128)} %convert_element_type.331, (f32[129,512]{1,0:T(8,128)S(1)}, f32[129,512]{1,0:T(8,128)S(1)}) %tuple.76, (pred[]{:T(512)}, s32[]{:T(128)}, pred[]{:T(512)}, bf16[4096,512]{1,0:T(8,128)(2,1)}, bf16[129,128]{1,0:T(8,128)(2,1)S(1)}, ...), branch_computations={%region_3.3_spmd, %region_4.6_spmd} | conditional | flops 136190976 | bytes 6068488 | solution.py:123
  394.5 8.9 %conditional.5 = ((f32[129,512]{1,0:T(8,128)S(1)}, f32[129,512]{1,0:T(8,128)S(1)})) conditional(s32[]{:T(128)} %convert_element_type.331, (f32[129,512]{1,0:T(8,128)S(1)}, f32[129,512]{1,0:T(8,128)S(1)}) %tuple.76, (pred[]{:T(512)}, s32[]{:T(128)}, pred[]{:T(512)}, bf16[4096,512]{1,0:T(8,128)(2,1)}, bf16[129,128]{1,0:T(8,128)(2,1)S(1)}, ...), branch_computations={%region_3.3_spmd, %region_4.6_spmd} | conditional | flops 136190976 | bytes 6068488 | solution.py:123
  398.9 4.5 conditional
  403.7 8.9 %conditional.5 = ((f32[129,512]{1,0:T(8,128)S(1)}, f32[129,512]{1,0:T(8,128)S(1)})) conditional(s32[]{:T(128)} %convert_element_type.331, (f32[129,512]{1,0:T(8,128)S(1)}, f32[129,512]{1,0:T(8,128)S(1)}) %tuple.76, (pred[]{:T(512)}, s32[]{:T(128)}, pred[]{:T(512)}, bf16[4096,512]{1,0:T(8,128)(2,1)}, bf16[129,128]{1,0:T(8,128)(2,1)S(1)}, ...), branch_computations={%region_3.3_spmd, %region_4.6_spmd} | conditional | flops 136190976 | bytes 6068488 | solution.py:123
  412.9 8.9 %conditional.5 = ((f32[129,512]{1,0:T(8,128)S(1)}, f32[129,512]{1,0:T(8,128)S(1)})) conditional(s32[]{:T(128)} %convert_element_type.331, (f32[129,512]{1,0:T(8,128)S(1)}, f32[129,512]{1,0:T(8,128)S(1)}) %tuple.76, (pred[]{:T(512)}, s32[]{:T(128)}, pred[]{:T(512)}, bf16[4096,512]{1,0:T(8,128)(2,1)}, bf16[129,128]{1,0:T(8,128)(2,1)S(1)}, ...), branch_computations={%region_3.3_spmd, %region_4.6_spmd} | conditional | flops 136190976 | bytes 6068488 | solution.py:123
  417.3 4.5 conditional
  422.1 8.9 %conditional.5 = ((f32[129,512]{1,0:T(8,128)S(1)}, f32[129,512]{1,0:T(8,128)S(1)})) conditional(s32[]{:T(128)} %convert_element_type.331, (f32[129,512]{1,0:T(8,128)S(1)}, f32[129,512]{1,0:T(8,128)S(1)}) %tuple.76, (pred[]{:T(512)}, s32[]{:T(128)}, pred[]{:T(512)}, bf16[4096,512]{1,0:T(8,128)(2,1)}, bf16[129,128]{1,0:T(8,128)(2,1)S(1)}, ...), branch_computations={%region_3.3_spmd, %region_4.6_spmd} | conditional | flops 136190976 | bytes 6068488 | solution.py:123
  431.4 8.9 %conditional.5 = ((f32[129,512]{1,0:T(8,128)S(1)}, f32[129,512]{1,0:T(8,128)S(1)})) conditional(s32[]{:T(128)} %convert_element_type.331, (f32[129,512]{1,0:T(8,128)S(1)}, f32[129,512]{1,0:T(8,128)S(1)}) %tuple.76, (pred[]{:T(512)}, s32[]{:T(128)}, pred[]{:T(512)}, bf16[4096,512]{1,0:T(8,128)(2,1)}, bf16[129,128]{1,0:T(8,128)(2,1)S(1)}, ...), branch_computations={%region_3.3_spmd, %region_4.6_spmd} | conditional | flops 136190976 | bytes 6068488 | solution.py:123
  440.6 8.9 %conditional.5 = ((f32[129,512]{1,0:T(8,128)S(1)}, f32[129,512]{1,0:T(8,128)S(1)})) conditional(s32[]{:T(128)} %convert_element_type.331, (f32[129,512]{1,0:T(8,128)S(1)}, f32[129,512]{1,0:T(8,128)S(1)}) %tuple.76, (pred[]{:T(512)}, s32[]{:T(128)}, pred[]{:T(512)}, bf16[4096,512]{1,0:T(8,128)(2,1)}, bf16[129,128]{1,0:T(8,128)(2,1)S(1)}, ...), branch_computations={%region_3.3_spmd, %region_4.6_spmd} | conditional | flops 136190976 | bytes 6068488 | solution.py:123
  (345 shorter events, 389.5 us)
Async XLA Ops:
  6.5 75.1 %all-gather.5.cloned.1.call-start = ((), (), s32[]{:S(2)}) async-start(), calls=%async_computation.1 | async-start | bytes 4325376 | tf_op jit(solution)/shard_map/all_gather | solution.py:77
  7.3 147.3 %all-gather.3.cloned.1.call-start = ((), (), s32[]{:S(2)}) async-start(), calls=%async_computation | async-start | bytes 4325376 | tf_op jit(solution)/shard_map/all_gather | solution.py:94
  449.6 4.8 %copy-start = (bf16[128,512]{1,0:T(8,128)(2,1)S(1)}, bf16[128,512]{1,0:T(8,128)(2,1)}, u32[]{:S(2)}) copy-start(bf16[128,512]{1,0:T(8,128)(2,1)} %fusion.35) | copy-start | bytes 393220
  449.7 4.8 %copy-start.1 = (bf16[128,512]{1,0:T(8,128)(2,1)S(1)}, bf16[128,512]{1,0:T(8,128)(2,1)}, u32[]{:S(2)}) copy-start(bf16[128,512]{1,0:T(8,128)(2,1)} %param.15) | copy-start | bytes 393220
  449.7 4.8 %copy-start.2 = (f32[512]{0:T(512)S(1)}, f32[512]{0:T(512)}, u32[]{:S(2)}) copy-start(f32[512]{0:T(512)} %param.13) | copy-start | bytes 6148
  451.2 3.2 collective-permute-start
Sparse Core Ops, SparseCore 0:
  9.5 72.1 all-gather.4
  83.8 70.7 all-gather.2
where the time goes:
time: 467 us; the launch traced here: 462 us
  matrix products  282 us (60%)
  waiting for transfers between devices  117 us (25%)
  blocking collectives  28.1 us (6%)
  other arithmetic  14.2 us (3%)
  between operations  13.6 us (3%)
  loops' own time  5.88 us (1%)
    dot_general x128, matrix products, table_dot(): jnp.dot(table_pair[1], data, preferred_element_type=jnp.float32)  141 us
    dot_general x128, matrix products, table_dot(): jnp.dot(table_pair[0], data, preferred_element_type=jnp.float32)  138 us
    all_gather x1, waiting for transfers between devices, local(): segment_in = lax.all_gather(normed, 'ctx', axis=0, tiled=True)  72.9 us
    all_gather x1, waiting for transfers between devices, local(): whole_filter = lax.all_gather(filter_taps, 'ctx', axis=0, tiled=True)  41.6 us
    psum x1, blocking collectives, local(): row_power = lax.psum(jnp.sum(values * values, axis=1), 'ch') / C  28.1 us
    convert_element_type x36, other arithmetic, split_parts(): high = matrix.astype(jnp.bfloat16)  10.1 us
  transfers between devices with their start and end apart: 3, of which 3 were waited for; matrix products, arithmetic and copies ran while one was open for 1% of the time, Pallas kernels for 0%

commit v1 on v0

--- a/solution.py
+++ b/solution.py
@@ -62,7 +62,7 @@
     ctx_count = lax.axis_size("ctx")
     ctx_index = lax.axis_index("ctx")
     values = signal.astype(jnp.float32)
-    row_power = lax.psum(jnp.sum(values * values, axis=1), "ch") / C
+    row_power = jnp.sum(lax.all_gather(jnp.sum(values * values, axis=1), "ch"), axis=0) / C
     normed = (values * lax.rsqrt(row_power + EPS)[:, None] * norm_gain[None, :]).astype(
         jnp.bfloat16
     )

time: 467 us -> 467 us (level)
  blocking collectives: 28.1 us -> 16 us
  waiting for transfers between devices: 117 us -> 129 us
    psum x1 -> x0, blocking collectives: 28.1 us -> none  [local(): row_power = lax.psum(jnp.sum(values * values, axis=1), 'ch') / C]
    all_gather x0 -> x1, blocking collectives: none -> 16 us  [local(): lax.all_gather(jnp.sum(values * values, axis=1), 'ch')]
    all_gather x1, waiting for transfers between devices: 41.6 us -> 53.4 us  [local(): whole_filter = lax.all_gather(filter_taps, 'ctx', axis=0, tiled=True)]
where the time goes in v1:
time: 467 us; the launch traced here: 462 us
  matrix products  282 us (60%)
  waiting for transfers between devices  129 us (28%)
  blocking collectives  16 us (3%)
  other arithmetic  14.2 us (3%)
  between operations  13.6 us (3%)
  loops' own time  5.88 us (1%)
    dot_general x128, matrix products, table_dot(): jnp.dot(table_pair[1], data, preferred_element_type=jnp.float32)  141 us
    dot_general x128, matrix products, table_dot(): jnp.dot(table_pair[0], data, preferred_element_type=jnp.float32)  138 us
    all_gather x1, waiting for transfers between devices, local(): segment_in = lax.all_gather(normed, 'ctx', axis=0, tiled=True)  73.1 us
    all_gather x1, waiting for transfers between devices, local(): whole_filter = lax.all_gather(filter_taps, 'ctx', axis=0, tiled=True)  53.4 us
    all_gather x1, blocking collectives, local(): lax.all_gather(jnp.sum(values * values, axis=1), 'ch')  16 us
    convert_element_type x36, other arithmetic, split_parts(): high = matrix.astype(jnp.bfloat16)  10.1 us
  transfers between devices with their start and end apart: 3, of which 3 were waited for; matrix products, arithmetic and copies ran while one was open for 1% of the time, Pallas kernels for 0%

profile of v1, /device:TPU:483, one launch (start us, length us, event | category | flops | bytes accessed | tf_op | source)
XLA Modules:
  0.0 462.2 jit_solution(11746377127055512951)
XLA Ops:
  8.3 16.0 %all-gather.1 = f32[16,1,128]{2,1,0:T(1,128)S(1)} all-gather(f32[1,1,128]{2,1,0:T(1,128)S(1)} %bitcast.37), channel_id=2, replica_groups=mesh['ctx'=32,'ch'=16] {'ch'}, dimensions={0}, use_global_device_ids=true | all-gather | bytes 8704 | tf_op jit(solution)/shard_map/all_gather | solution.py:65
  28.1 53.4 %all-gather.7.cloned.1.call-done = bf16[4096,512]{1,0:T(8,128)(2,1)} async-done(((bf16[128,512]{1,0:T(8,128)(2,1)}), bf16[4096,512]{1,0:T(8,128)(2,1)}) %all-gather.7.cloned.1.call-update) | async-done | bytes 4194320 | tf_op jit(solution)/shard_map/all_gather | solution.py:77
  81.5 73.1 %all-gather.5.cloned.1.call-done = bf16[4096,512]{1,0:T(8,128)(2,1)} async-done(((bf16[128,512]{1,0:T(8,128)(2,1)}), bf16[4096,512]{1,0:T(8,128)(2,1)}) %all-gather.5.cloned.1.call-update) | async-done | bytes 4194320 | tf_op jit(solution)/shard_map/all_gather | solution.py:94
  154.6 294.8 %while.19 = (s32[]{:T(128)}, f32[129,512]{1,0:T(8,128)S(1)}, f32[129,512]{1,0:T(8,128)S(1)}, s32[]{:T(128)}, bf16[4096,512]{1,0:T(8,128)(2,1)}, /*index=5*/bf16[...) while((s32[]{:T(128)}, f32[129,512]{1,0:T(8,128)S(1)}, ...), condition=%wide.region_7.8_spmd.clone.clone, body=%wide.region_2.7_spmd.clone.clone.sunk | while | flops 136455184 | bytes 6134993 | solution.py:125
  155.0 8.9 %conditional.5 = ((f32[129,512]{1,0:T(8,128)S(1)}, f32[129,512]{1,0:T(8,128)S(1)})) conditional(s32[]{:T(128)} %convert_element_type.331, (f32[129,512]{1,0:T(8,128)S(1)}, f32[129,512]{1,0:T(8,128)S(1)}) %tuple.76, (pred[]{:T(512)}, s32[]{:T(128)}, pred[]{:T(512)}, bf16[4096,512]{1,0:T(8,128)(2,1)}, bf16[129,128]{1,0:T(8,128)(2,1)S(1)}, ...), branch_computations={%region_3.3_spmd, %region_4.6_spmd} | conditional | flops 136190976 | bytes 6068488 | solution.py:123
  159.4 4.5 conditional
  164.2 8.9 %conditional.5 = ((f32[129,512]{1,0:T(8,128)S(1)}, f32[129,512]{1,0:T(8,128)S(1)})) conditional(s32[]{:T(128)} %convert_element_type.331, (f32[129,512]{1,0:T(8,128)S(1)}, f32[129,512]{1,0:T(8,128)S(1)}) %tuple.76, (pred[]{:T(512)}, s32[]{:T(128)}, pred[]{:T(512)}, bf16[4096,512]{1,0:T(8,128)(2,1)}, bf16[129,128]{1,0:T(8,128)(2,1)S(1)}, ...), branch_computations={%region_3.3_spmd, %region_4.6_spmd} | conditional | flops 136190976 | bytes 6068488 | solution.py:123
  173.4 8.9 %conditional.5 = ((f32[129,512]{1,0:T(8,128)S(1)}, f32[129,512]{1,0:T(8,128)S(1)})) conditional(s32[]{:T(128)} %convert_element_type.331, (f32[129,512]{1,0:T(8,128)S(1)}, f32[129,512]{1,0:T(8,128)S(1)}) %tuple.76, (pred[]{:T(512)}, s32[]{:T(128)}, pred[]{:T(512)}, bf16[4096,512]{1,0:T(8,128)(2,1)}, bf16[129,128]{1,0:T(8,128)(2,1)S(1)}, ...), branch_computations={%region_3.3_spmd, %region_4.6_spmd} | conditional | flops 136190976 | bytes 6068488 | solution.py:123
  177.8 4.5 conditional
  182.6 8.9 %conditional.5 = ((f32[129,512]{1,0:T(8,128)S(1)}, f32[129,512]{1,0:T(8,128)S(1)})) conditional(s32[]{:T(128)} %convert_element_type.331, (f32[129,512]{1,0:T(8,128)S(1)}, f32[129,512]{1,0:T(8,128)S(1)}) %tuple.76, (pred[]{:T(512)}, s32[]{:T(128)}, pred[]{:T(512)}, bf16[4096,512]{1,0:T(8,128)(2,1)}, bf16[129,128]{1,0:T(8,128)(2,1)S(1)}, ...), branch_computations={%region_3.3_spmd, %region_4.6_spmd} | conditional | flops 136190976 | bytes 6068488 | solution.py:123
  191.8 8.9 %conditional.5 = ((f32[129,512]{1,0:T(8,128)S(1)}, f32[129,512]{1,0:T(8,128)S(1)})) conditional(s32[]{:T(128)} %convert_element_type.331, (f32[129,512]{1,0:T(8,128)S(1)}, f32[129,512]{1,0:T(8,128)S(1)}) %tuple.76, (pred[]{:T(512)}, s32[]{:T(128)}, pred[]{:T(512)}, bf16[4096,512]{1,0:T(8,128)(2,1)}, bf16[129,128]{1,0:T(8,128)(2,1)S(1)}, ...), branch_computations={%region_3.3_spmd, %region_4.6_spmd} | conditional | flops 136190976 | bytes 6068488 | solution.py:123
  201.0 8.9 %conditional.5 = ((f32[129,512]{1,0:T(8,128)S(1)}, f32[129,512]{1,0:T(8,128)S(1)})) conditional(s32[]{:T(128)} %convert_element_type.331, (f32[129,512]{1,0:T(8,128)S(1)}, f32[129,512]{1,0:T(8,128)S(1)}) %tuple.76, (pred[]{:T(512)}, s32[]{:T(128)}, pred[]{:T(512)}, bf16[4096,512]{1,0:T(8,128)(2,1)}, bf16[129,128]{1,0:T(8,128)(2,1)S(1)}, ...), branch_computations={%region_3.3_spmd, %region_4.6_spmd} | conditional | flops 136190976 | bytes 6068488 | solution.py:123
  205.4 4.5 conditional
  210.3 8.9 %conditional.5 = ((f32[129,512]{1,0:T(8,128)S(1)}, f32[129,512]{1,0:T(8,128)S(1)})) conditional(s32[]{:T(128)} %convert_element_type.331, (f32[129,512]{1,0:T(8,128)S(1)}, f32[129,512]{1,0:T(8,128)S(1)}) %tuple.76, (pred[]{:T(512)}, s32[]{:T(128)}, pred[]{:T(512)}, bf16[4096,512]{1,0:T(8,128)(2,1)}, bf16[129,128]{1,0:T(8,128)(2,1)S(1)}, ...), branch_computations={%region_3.3_spmd, %region_4.6_spmd} | conditional | flops 136190976 | bytes 6068488 | solution.py:123
  219.5 8.9 %conditional.5 = ((f32[129,512]{1,0:T(8,128)S(1)}, f32[129,512]{1,0:T(8,128)S(1)})) conditional(s32[]{:T(128)} %convert_element_type.331, (f32[129,512]{1,0:T(8,128)S(1)}, f32[129,512]{1,0:T(8,128)S(1)}) %tuple.76, (pred[]{:T(512)}, s32[]{:T(128)}, pred[]{:T(512)}, bf16[4096,512]{1,0:T(8,128)(2,1)}, bf16[129,128]{1,0:T(8,128)(2,1)S(1)}, ...), branch_computations={%region_3.3_spmd, %region_4.6_spmd} | conditional | flops 136190976 | bytes 6068488 | solution.py:123
  223.8 4.5 conditional
  228.7 8.9 %conditional.5 = ((f32[129,512]{1,0:T(8,128)S(1)}, f32[129,512]{1,0:T(8,128)S(1)})) conditional(s32[]{:T(128)} %convert_element_type.331, (f32[129,512]{1,0:T(8,128)S(1)}, f32[129,512]{1,0:T(8,128)S(1)}) %tuple.76, (pred[]{:T(512)}, s32[]{:T(128)}, pred[]{:T(512)}, bf16[4096,512]{1,0:T(8,128)(2,1)}, bf16[129,128]{1,0:T(8,128)(2,1)S(1)}, ...), branch_computations={%region_3.3_spmd, %region_4.6_spmd} | conditional | flops 136190976 | bytes 6068488 | solution.py:123
  237.9 8.9 %conditional.5 = ((f32[129,512]{1,0:T(8,128)S(1)}, f32[129,512]{1,0:T(8,128)S(1)})) conditional(s32[]{:T(128)} %convert_element_type.331, (f32[129,512]{1,0:T(8,128)S(1)}, f32[129,512]{1,0:T(8,128)S(1)}) %tuple.76, (pred[]{:T(512)}, s32[]{:T(128)}, pred[]{:T(512)}, bf16[4096,512]{1,0:T(8,128)(2,1)}, bf16[129,128]{1,0:T(8,128)(2,1)S(1)}, ...), branch_computations={%region_3.3_spmd, %region_4.6_spmd} | conditional | flops 136190976 | bytes 6068488 | solution.py:123
  242.3 4.5 conditional
  247.1 8.9 %conditional.5 = ((f32[129,512]{1,0:T(8,128)S(1)}, f32[129,512]{1,0:T(8,128)S(1)})) conditional(s32[]{:T(128)} %convert_element_type.331, (f32[129,512]{1,0:T(8,128)S(1)}, f32[129,512]{1,0:T(8,128)S(1)}) %tuple.76, (pred[]{:T(512)}, s32[]{:T(128)}, pred[]{:T(512)}, bf16[4096,512]{1,0:T(8,128)(2,1)}, bf16[129,128]{1,0:T(8,128)(2,1)S(1)}, ...), branch_computations={%region_3.3_spmd, %region_4.6_spmd} | conditional | flops 136190976 | bytes 6068488 | solution.py:123
  256.3 8.9 %conditional.5 = ((f32[129,512]{1,0:T(8,128)S(1)}, f32[129,512]{1,0:T(8,128)S(1)})) conditional(s32[]{:T(128)} %convert_element_type.331, (f32[129,512]{1,0:T(8,128)S(1)}, f32[129,512]{1,0:T(8,128)S(1)}) %tuple.76, (pred[]{:T(512)}, s32[]{:T(128)}, pred[]{:T(512)}, bf16[4096,512]{1,0:T(8,128)(2,1)}, bf16[129,128]{1,0:T(8,128)(2,1)S(1)}, ...), branch_computations={%region_3.3_spmd, %region_4.6_spmd} | conditional | flops 136190976 | bytes 6068488 | solution.py:123
  265.5 8.9 %conditional.5 = ((f32[129,512]{1,0:T(8,128)S(1)}, f32[129,512]{1,0:T(8,128)S(1)})) conditional(s32[]{:T(128)} %convert_element_type.331, (f32[129,512]{1,0:T(8,128)S(1)}, f32[129,512]{1,0:T(8,128)S(1)}) %tuple.76, (pred[]{:T(512)}, s32[]{:T(128)}, pred[]{:T(512)}, bf16[4096,512]{1,0:T(8,128)(2,1)}, bf16[129,128]{1,0:T(8,128)(2,1)S(1)}, ...), branch_computations={%region_3.3_spmd, %region_4.6_spmd} | conditional | flops 136190976 | bytes 6068488 | solution.py:123
  269.9 4.5 conditional
  274.7 8.9 %conditional.5 = ((f32[129,512]{1,0:T(8,128)S(1)}, f32[129,512]{1,0:T(8,128)S(1)})) conditional(s32[]{:T(128)} %convert_element_type.331, (f32[129,512]{1,0:T(8,128)S(1)}, f32[129,512]{1,0:T(8,128)S(1)}) %tuple.76, (pred[]{:T(512)}, s32[]{:T(128)}, pred[]{:T(512)}, bf16[4096,512]{1,0:T(8,128)(2,1)}, bf16[129,128]{1,0:T(8,128)(2,1)S(1)}, ...), branch_computations={%region_3.3_spmd, %region_4.6_spmd} | conditional | flops 136190976 | bytes 6068488 | solution.py:123
  284.0 8.9 %conditional.5 = ((f32[129,512]{1,0:T(8,128)S(1)}, f32[129,512]{1,0:T(8,128)S(1)})) conditional(s32[]{:T(128)} %convert_element_type.331, (f32[129,512]{1,0:T(8,128)S(1)}, f32[129,512]{1,0:T(8,128)S(1)}) %tuple.76, (pred[]{:T(512)}, s32[]{:T(128)}, pred[]{:T(512)}, bf16[4096,512]{1,0:T(8,128)(2,1)}, bf16[129,128]{1,0:T(8,128)(2,1)S(1)}, ...), branch_computations={%region_3.3_spmd, %region_4.6_spmd} | conditional | flops 136190976 | bytes 6068488 | solution.py:123
  288.3 4.5 conditional
  293.2 8.9 %conditional.5 = ((f32[129,512]{1,0:T(8,128)S(1)}, f32[129,512]{1,0:T(8,128)S(1)})) conditional(s32[]{:T(128)} %convert_element_type.331, (f32[129,512]{1,0:T(8,128)S(1)}, f32[129,512]{1,0:T(8,128)S(1)}) %tuple.76, (pred[]{:T(512)}, s32[]{:T(128)}, pred[]{:T(512)}, bf16[4096,512]{1,0:T(8,128)(2,1)}, bf16[129,128]{1,0:T(8,128)(2,1)S(1)}, ...), branch_computations={%region_3.3_spmd, %region_4.6_spmd} | conditional | flops 136190976 | bytes 6068488 | solution.py:123
  302.4 8.9 %conditional.5 = ((f32[129,512]{1,0:T(8,128)S(1)}, f32[129,512]{1,0:T(8,128)S(1)})) conditional(s32[]{:T(128)} %convert_element_type.331, (f32[129,512]{1,0:T(8,128)S(1)}, f32[129,512]{1,0:T(8,128)S(1)}) %tuple.76, (pred[]{:T(512)}, s32[]{:T(128)}, pred[]{:T(512)}, bf16[4096,512]{1,0:T(8,128)(2,1)}, bf16[129,128]{1,0:T(8,128)(2,1)S(1)}, ...), branch_computations={%region_3.3_spmd, %region_4.6_spmd} | conditional | flops 136190976 | bytes 6068488 | solution.py:123
  311.6 8.9 %conditional.5 = ((f32[129,512]{1,0:T(8,128)S(1)}, f32[129,512]{1,0:T(8,128)S(1)})) conditional(s32[]{:T(128)} %convert_element_type.331, (f32[129,512]{1,0:T(8,128)S(1)}, f32[129,512]{1,0:T(8,128)S(1)}) %tuple.76, (pred[]{:T(512)}, s32[]{:T(128)}, pred[]{:T(512)}, bf16[4096,512]{1,0:T(8,128)(2,1)}, bf16[129,128]{1,0:T(8,128)(2,1)S(1)}, ...), branch_computations={%region_3.3_spmd, %region_4.6_spmd} | conditional | flops 136190976 | bytes 6068488 | solution.py:123
  320.8 8.9 %conditional.5 = ((f32[129,512]{1,0:T(8,128)S(1)}, f32[129,512]{1,0:T(8,128)S(1)})) conditional(s32[]{:T(128)} %convert_element_type.331, (f32[129,512]{1,0:T(8,128)S(1)}, f32[129,512]{1,0:T(8,128)S(1)}) %tuple.76, (pred[]{:T(512)}, s32[]{:T(128)}, pred[]{:T(512)}, bf16[4096,512]{1,0:T(8,128)(2,1)}, bf16[129,128]{1,0:T(8,128)(2,1)S(1)}, ...), branch_computations={%region_3.3_spmd, %region_4.6_spmd} | conditional | flops 136190976 | bytes 6068488 | solution.py:123
  330.0 8.9 %conditional.5 = ((f32[129,512]{1,0:T(8,128)S(1)}, f32[129,512]{1,0:T(8,128)S(1)})) conditional(s32[]{:T(128)} %convert_element_type.331, (f32[129,512]{1,0:T(8,128)S(1)}, f32[129,512]{1,0:T(8,128)S(1)}) %tuple.76, (pred[]{:T(512)}, s32[]{:T(128)}, pred[]{:T(512)}, bf16[4096,512]{1,0:T(8,128)(2,1)}, bf16[129,128]{1,0:T(8,128)(2,1)S(1)}, ...), branch_computations={%region_3.3_spmd, %region_4.6_spmd} | conditional | flops 136190976 | bytes 6068488 | solution.py:123
  334.4 4.5 conditional
  339.2 8.9 %conditional.5 = ((f32[129,512]{1,0:T(8,128)S(1)}, f32[129,512]{1,0:T(8,128)S(1)})) conditional(s32[]{:T(128)} %convert_element_type.331, (f32[129,512]{1,0:T(8,128)S(1)}, f32[129,512]{1,0:T(8,128)S(1)}) %tuple.76, (pred[]{:T(512)}, s32[]{:T(128)}, pred[]{:T(512)}, bf16[4096,512]{1,0:T(8,128)(2,1)}, bf16[129,128]{1,0:T(8,128)(2,1)S(1)}, ...), branch_computations={%region_3.3_spmd, %region_4.6_spmd} | conditional | flops 136190976 | bytes 6068488 | solution.py:123
  348.4 8.9 %conditional.5 = ((f32[129,512]{1,0:T(8,128)S(1)}, f32[129,512]{1,0:T(8,128)S(1)})) conditional(s32[]{:T(128)} %convert_element_type.331, (f32[129,512]{1,0:T(8,128)S(1)}, f32[129,512]{1,0:T(8,128)S(1)}) %tuple.76, (pred[]{:T(512)}, s32[]{:T(128)}, pred[]{:T(512)}, bf16[4096,512]{1,0:T(8,128)(2,1)}, bf16[129,128]{1,0:T(8,128)(2,1)S(1)}, ...), branch_computations={%region_3.3_spmd, %region_4.6_spmd} | conditional | flops 136190976 | bytes 6068488 | solution.py:123
  352.8 4.5 conditional
  357.7 8.9 %conditional.5 = ((f32[129,512]{1,0:T(8,128)S(1)}, f32[129,512]{1,0:T(8,128)S(1)})) conditional(s32[]{:T(128)} %convert_element_type.331, (f32[129,512]{1,0:T(8,128)S(1)}, f32[129,512]{1,0:T(8,128)S(1)}) %tuple.76, (pred[]{:T(512)}, s32[]{:T(128)}, pred[]{:T(512)}, bf16[4096,512]{1,0:T(8,128)(2,1)}, bf16[129,128]{1,0:T(8,128)(2,1)S(1)}, ...), branch_computations={%region_3.3_spmd, %region_4.6_spmd} | conditional | flops 136190976 | bytes 6068488 | solution.py:123
  366.9 8.9 %conditional.5 = ((f32[129,512]{1,0:T(8,128)S(1)}, f32[129,512]{1,0:T(8,128)S(1)})) conditional(s32[]{:T(128)} %convert_element_type.331, (f32[129,512]{1,0:T(8,128)S(1)}, f32[129,512]{1,0:T(8,128)S(1)}) %tuple.76, (pred[]{:T(512)}, s32[]{:T(128)}, pred[]{:T(512)}, bf16[4096,512]{1,0:T(8,128)(2,1)}, bf16[129,128]{1,0:T(8,128)(2,1)S(1)}, ...), branch_computations={%region_3.3_spmd, %region_4.6_spmd} | conditional | flops 136190976 | bytes 6068488 | solution.py:123
  376.1 8.9 %conditional.5 = ((f32[129,512]{1,0:T(8,128)S(1)}, f32[129,512]{1,0:T(8,128)S(1)})) conditional(s32[]{:T(128)} %convert_element_type.331, (f32[129,512]{1,0:T(8,128)S(1)}, f32[129,512]{1,0:T(8,128)S(1)}) %tuple.76, (pred[]{:T(512)}, s32[]{:T(128)}, pred[]{:T(512)}, bf16[4096,512]{1,0:T(8,128)(2,1)}, bf16[129,128]{1,0:T(8,128)(2,1)S(1)}, ...), branch_computations={%region_3.3_spmd, %region_4.6_spmd} | conditional | flops 136190976 | bytes 6068488 | solution.py:123
  380.5 4.5 conditional
  385.3 8.9 %conditional.5 = ((f32[129,512]{1,0:T(8,128)S(1)}, f32[129,512]{1,0:T(8,128)S(1)})) conditional(s32[]{:T(128)} %convert_element_type.331, (f32[129,512]{1,0:T(8,128)S(1)}, f32[129,512]{1,0:T(8,128)S(1)}) %tuple.76, (pred[]{:T(512)}, s32[]{:T(128)}, pred[]{:T(512)}, bf16[4096,512]{1,0:T(8,128)(2,1)}, bf16[129,128]{1,0:T(8,128)(2,1)S(1)}, ...), branch_computations={%region_3.3_spmd, %region_4.6_spmd} | conditional | flops 136190976 | bytes 6068488 | solution.py:123
  394.5 8.9 %conditional.5 = ((f32[129,512]{1,0:T(8,128)S(1)}, f32[129,512]{1,0:T(8,128)S(1)})) conditional(s32[]{:T(128)} %convert_element_type.331, (f32[129,512]{1,0:T(8,128)S(1)}, f32[129,512]{1,0:T(8,128)S(1)}) %tuple.76, (pred[]{:T(512)}, s32[]{:T(128)}, pred[]{:T(512)}, bf16[4096,512]{1,0:T(8,128)(2,1)}, bf16[129,128]{1,0:T(8,128)(2,1)S(1)}, ...), branch_computations={%region_3.3_spmd, %region_4.6_spmd} | conditional | flops 136190976 | bytes 6068488 | solution.py:123
  398.9 4.5 conditional
  403.7 8.9 %conditional.5 = ((f32[129,512]{1,0:T(8,128)S(1)}, f32[129,512]{1,0:T(8,128)S(1)})) conditional(s32[]{:T(128)} %convert_element_type.331, (f32[129,512]{1,0:T(8,128)S(1)}, f32[129,512]{1,0:T(8,128)S(1)}) %tuple.76, (pred[]{:T(512)}, s32[]{:T(128)}, pred[]{:T(512)}, bf16[4096,512]{1,0:T(8,128)(2,1)}, bf16[129,128]{1,0:T(8,128)(2,1)S(1)}, ...), branch_computations={%region_3.3_spmd, %region_4.6_spmd} | conditional | flops 136190976 | bytes 6068488 | solution.py:123
  412.9 8.9 %conditional.5 = ((f32[129,512]{1,0:T(8,128)S(1)}, f32[129,512]{1,0:T(8,128)S(1)})) conditional(s32[]{:T(128)} %convert_element_type.331, (f32[129,512]{1,0:T(8,128)S(1)}, f32[129,512]{1,0:T(8,128)S(1)}) %tuple.76, (pred[]{:T(512)}, s32[]{:T(128)}, pred[]{:T(512)}, bf16[4096,512]{1,0:T(8,128)(2,1)}, bf16[129,128]{1,0:T(8,128)(2,1)S(1)}, ...), branch_computations={%region_3.3_spmd, %region_4.6_spmd} | conditional | flops 136190976 | bytes 6068488 | solution.py:123
  417.3 4.5 conditional
  422.1 8.9 %conditional.5 = ((f32[129,512]{1,0:T(8,128)S(1)}, f32[129,512]{1,0:T(8,128)S(1)})) conditional(s32[]{:T(128)} %convert_element_type.331, (f32[129,512]{1,0:T(8,128)S(1)}, f32[129,512]{1,0:T(8,128)S(1)}) %tuple.76, (pred[]{:T(512)}, s32[]{:T(128)}, pred[]{:T(512)}, bf16[4096,512]{1,0:T(8,128)(2,1)}, bf16[129,128]{1,0:T(8,128)(2,1)S(1)}, ...), branch_computations={%region_3.3_spmd, %region_4.6_spmd} | conditional | flops 136190976 | bytes 6068488 | solution.py:123
  431.4 8.9 %conditional.5 = ((f32[129,512]{1,0:T(8,128)S(1)}, f32[129,512]{1,0:T(8,128)S(1)})) conditional(s32[]{:T(128)} %convert_element_type.331, (f32[129,512]{1,0:T(8,128)S(1)}, f32[129,512]{1,0:T(8,128)S(1)}) %tuple.76, (pred[]{:T(512)}, s32[]{:T(128)}, pred[]{:T(512)}, bf16[4096,512]{1,0:T(8,128)(2,1)}, bf16[129,128]{1,0:T(8,128)(2,1)S(1)}, ...), branch_computations={%region_3.3_spmd, %region_4.6_spmd} | conditional | flops 136190976 | bytes 6068488 | solution.py:123
  440.6 8.9 %conditional.5 = ((f32[129,512]{1,0:T(8,128)S(1)}, f32[129,512]{1,0:T(8,128)S(1)})) conditional(s32[]{:T(128)} %convert_element_type.331, (f32[129,512]{1,0:T(8,128)S(1)}, f32[129,512]{1,0:T(8,128)S(1)}) %tuple.76, (pred[]{:T(512)}, s32[]{:T(128)}, pred[]{:T(512)}, bf16[4096,512]{1,0:T(8,128)(2,1)}, bf16[129,128]{1,0:T(8,128)(2,1)S(1)}, ...), branch_computations={%region_3.3_spmd, %region_4.6_spmd} | conditional | flops 136190976 | bytes 6068488 | solution.py:123
  (346 shorter events, 389.5 us)
Async XLA Ops:
  6.5 74.9 %all-gather.7.cloned.1.call-start = ((), (), s32[]{:S(2)}) async-start(), calls=%async_computation.1 | async-start | bytes 4325376 | tf_op jit(solution)/shard_map/all_gather | solution.py:77
  7.3 147.3 %all-gather.5.cloned.1.call-start = ((), (), s32[]{:S(2)}) async-start(), calls=%async_computation | async-start | bytes 4325376 | tf_op jit(solution)/shard_map/all_gather | solution.py:94
  449.6 4.8 %copy-start = (bf16[128,512]{1,0:T(8,128)(2,1)S(1)}, bf16[128,512]{1,0:T(8,128)(2,1)}, u32[]{:S(2)}) copy-start(bf16[128,512]{1,0:T(8,128)(2,1)} %fusion.35) | copy-start | bytes 393220
  449.7 4.8 %copy-start.1 = (bf16[128,512]{1,0:T(8,128)(2,1)S(1)}, bf16[128,512]{1,0:T(8,128)(2,1)}, u32[]{:S(2)}) copy-start(bf16[128,512]{1,0:T(8,128)(2,1)} %param.15) | copy-start | bytes 393220
  449.7 4.8 %copy-start.2 = (f32[512]{0:T(512)S(1)}, f32[512]{0:T(512)}, u32[]{:S(2)}) copy-start(f32[512]{0:T(512)} %param.13) | copy-start | bytes 6148
  451.2 3.2 collective-permute-start
Sparse Core Ops, SparseCore 0:
  9.5 71.9 all-gather.6
  83.6 70.9 all-gather.4
